TPU v7x, 512 devices: a whole 4x4x16 slice. The times are simulated.
512 devices in a mesh: row: 32 (over y, z_hi, core), col: 16 (over z_lo, x).
Axes of the slice: x: 4, y: 4, z: 16 (z_hi: 4, z_lo: 4; z = z_hi * 4 + z_lo), core: 2. Of those that a mesh axis runs over, the one named last changes fastest.
Arguments:
- forcing_terms: float32 [32, 16, 2, 32, 128], P('row', 'col'), may hold values from -6 to 6
- diagonal_reciprocal: float32 [32, 16, 2, 128, 128], P('row', 'col'), may hold values from -0.5 to 0.5
- stiffness_submatrix: float32 [32, 16, 32, 128, 128], P('row', 'col'), may hold values from -0.1875 to 0.1875
- stiffness_source_index: int32 [32, 16, 32], P('row', 'col'), may hold values from 0 to 31
- stiffness_target_index: int32 [32, 16, 32], P('row', 'col'), may hold values from 0 to 63
- stiffness_nonzero_tally: int32 [32, 16], P('row', 'col'), may hold values from 1 to 32, as said below
- interpolant_submatrix: float32 [32, 16, 16, 128, 128], P('row', 'col'), may hold values from -0.0625 to 0.0625
- interpolant_cluster_index: int32 [32, 16, 16], P('row', 'col'), may hold values from 0 to 1
- interpolant_target_index: int32 [32, 16, 16], P('row', 'col'), may hold values from 0 to 63
- interpolant_nonzero_tally: int32 [32, 16], P('row', 'col'), may hold values from 1 to 16, as said below
- provisional_interpolant: float32 [32, 16, 2, 128], P('row', 'col'), may hold values from 0.2 to 1
- cluster_label: int32 [32, 16, 2, 128], P('row', 'col'), may hold values from 0 to 255
Outputs:
- relaxed_iterate: float32 [32, 16, 2, 32, 128], P('row', 'col')
- residual: float32 [32, 16, 2, 32, 128], P('row', 'col')
- coarse: float32 [32, 2, 32, 128], P('row')
Inputs may be any that keep to these rules, and one draw needn't show every extreme that they name: `stiffness_nonzero_tally`: tile slots at or past the count are unused; some pair has all 32 slots live in every draw. `interpolant_nonzero_tally`: tile slots at or past the count are unused; some pair has all 16 slots live in every draw.
All inputs are finite; a program needn't handle non-finite values.
Results may differ from a plain program's by a relative error of at most 0.0003.
Values sent between devices are 32-bit elements; how exact they have to be, the bound alone decides.
No kernel may reach another device: no remote copies, remote signals or barrier semaphores. Data moves between devices by JAX's collectives and lax.ppermute only.
A program may use at most 64 MiB of HBM per device.

v0:
```python
import jax
import jax.numpy as jnp
from jax import lax
from jax.sharding import PartitionSpec as P

omega = 0.7
highest = lax.Precision.HIGHEST
tile_group = 8


def loop_tiles(blocks, stiffness_submatrices, rows, cols, low, high, nout):
    nrhs = blocks.shape[1]
    width = blocks.shape[2]

    def add_group(index, total):
        start = index * tile_group
        piece = lax.dynamic_slice_in_dim(stiffness_submatrices, start, tile_group, 0)
        row_ids = lax.dynamic_slice_in_dim(rows, start, tile_group, 0)
        col_ids = lax.dynamic_slice_in_dim(cols, start, tile_group, 0)
        slots = start + jnp.arange(tile_group)
        live = ((slots >= low) & (slots < high)).astype(jnp.float32)
        inputs = jnp.take(blocks, col_ids, axis=0)
        product = jnp.einsum("ska,sab->skb", inputs, piece, precision=highest)
        onehot = (row_ids[:, None] == jnp.arange(nout)[None, :]).astype(jnp.float32) * live[:, None]
        return total + jnp.einsum("so,skb->okb", onehot, product, precision=highest)

    starting_guess = low // tile_group
    last = (high + tile_group - 1) // tile_group
    empty = jnp.zeros((nout, nrhs, width), jnp.float32)
    return lax.fori_loop(starting_guess, last, add_group, empty)


def gather_columns(vec):
    whole = lax.all_gather(vec[None, None], "row", axis=0, tiled=True)
    return whole.reshape(-1, vec.shape[1], vec.shape[2])


def precondition(vec, inverse):
    return jnp.einsum("pka,pab->pkb", vec, inverse, precision=highest)


def stiffness_product(vec, stiffness_submatrices, rows, cols, count):
    blocks = gather_columns(vec)
    ncol = lax.axis_size("col")
    pblocks = vec.shape[0]
    nout = ncol * pblocks
    partial_value = loop_tiles(blocks, stiffness_submatrices, rows, cols, jnp.int32(0), count, nout)
    partial_value = partial_value.reshape(1, ncol, pblocks, vec.shape[1], vec.shape[2])
    summed = lax.psum_scatter(partial_value, "col", scatter_dimension=1, tiled=True)
    return summed[0, 0]


def body(
    forcing_terms,
    diagonal_reciprocal,
    stiffness_submatrix,
    stiffness_source_index,
    stiffness_target_index,
    stiffness_nonzero_tally,
    interpolant_submatrix,
    interpolant_cluster_index,
    interpolant_target_index,
    interpolant_nonzero_tally,
    provisional_interpolant,
    cluster_label,
):
    source = forcing_terms[0, 0]
    inverse = diagonal_reciprocal[0, 0]
    stiffness_submatrices = stiffness_submatrix[0, 0]
    rows = stiffness_source_index[0, 0]
    cols = stiffness_target_index[0, 0]
    count = stiffness_nonzero_tally[0, 0]
    starting_guess = omega * precondition(source, inverse)
    image_field = stiffness_product(starting_guess, stiffness_submatrices, rows, cols, count)
    relaxed_iterate = starting_guess + omega * precondition(source - image_field, inverse)
    image_field = stiffness_product(relaxed_iterate, stiffness_submatrices, rows, cols, count)
    residual = source - image_field
    pblocks, nrhs, width = residual.shape
    blocks = gather_columns(residual)
    part = loop_tiles(
        blocks,
        interpolant_submatrix[0, 0],
        interpolant_cluster_index[0, 0],
        interpolant_target_index[0, 0],
        jnp.int32(0),
        interpolant_nonzero_tally[0, 0],
        pblocks,
    )
    weighted = (
        (residual * provisional_interpolant[0, 0][:, None, :])
        .transpose(1, 0, 2)
        .reshape(nrhs, pblocks * width)
    )
    onehot = (
        cluster_label[0, 0].reshape(-1)[:, None] == jnp.arange(pblocks * width)[None, :]
    ).astype(jnp.float32)
    tentative = jnp.dot(weighted, onehot, precision=highest)
    part = part + tentative.reshape(nrhs, pblocks, width).transpose(1, 0, 2)
    coarse = lax.psum(part, "col")
    return (relaxed_iterate[None, None], residual[None, None], coarse[None])


def solution(mesh):
    placed = (
        P("row", "col", None, None, None),
        P("row", "col", None, None, None),
        P("row", "col", None, None, None),
        P("row", "col", None),
        P("row", "col", None),
        P("row", "col"),
        P("row", "col", None, None, None),
        P("row", "col", None),
        P("row", "col", None),
        P("row", "col"),
        P("row", "col", None, None),
        P("row", "col", None, None),
    )
    return jax.shard_map(
        body,
        mesh=mesh,
        in_specs=placed,
        out_specs=(
            P("row", "col", None, None, None),
            P("row", "col", None, None, None),
            P("row", None, None, None),
        ),
        check_vma=False,
    )
```

profile of v0, /device:TPU:8, one launch (start us, length us, event | category | flops | bytes accessed | tf_op | source)
XLA Modules:
  0.0 539.8 jit_solution(16684769150870673594)
XLA Ops:
  7.2 0.8 copy-done
  8.1 1.6 convolution_multiply_fusion.1
  10.4 76.2 %all-gather.8.cloned.1.call-done = f32[64,32,128]{2,1,0:T(8,128)} async-done(((f32[2,32,128]{2,1,0:T(8,128)}), f32[64,32,128]{2,1,0:T(8,128)}) %all-gather.8.cloned.1.call-update) | async-done | bytes 1048592 | tf_op jit(solution)/shard_map/all_gather | solution.py:34
  86.7 19.1 %while.30 = (s32[]{:T(128)}, f32[32,32,128]{2,0,1:T(8,128)S(1)}, s32[]{:T(128)}, s32[32]{0:T(128)}, s32[]{:T(128)}, /*index=5*/s32[32]{0:T(128)}, f32[64,32,128]...) while((s32[]{:T(128)}, f32[32,32,128]{2,0,1:T(8,128)S(1)}, ...), condition=%wide.region_1.3_spmd, body=%wide.region_0.2_spmd.sunk | while | flops 63080028 | bytes 2232807 | solution.py:30
  86.7 1.4 compare_and_fusion.6
  88.1 1.8 gather_fusion
  89.9 1.7 fusion.75
  91.6 0.7 dynamic_slice.46
  92.3 0.8 convolution_add_fusion.6
  93.1 1.4 compare_and_fusion.6
  94.5 1.8 gather_fusion
  96.3 1.7 fusion.75
  97.9 0.7 dynamic_slice.46
  98.7 0.8 convolution_add_fusion.6
  99.5 1.4 compare_and_fusion.6
  100.9 1.8 gather_fusion
  102.7 1.7 fusion.75
  104.3 0.7 dynamic_slice.46
  105.0 0.8 convolution_add_fusion.6
  105.9 1.1 copy.25
  107.1 91.7 %reduce-scatter.3.cloned.1.call-done = f32[1,1,2,32,128]{4,3,2,1,0:T(8,128)} async-done(((f32[1,16,2,32,128]{4,3,2,1,0:T(8,128)}), f32[1,1,2,32,128]{4,3,2,1,0:T(8,128)}) %reduce-scatter.3.cloned.1.call-update) | async-done | bytes 32784 | tf_op jit(solution)/shard_map/reduce_scatter | solution.py:49
  198.8 1.6 fusion.45
  200.5 68.7 %all-gather.10.cloned.1.call-done = f32[64,32,128]{2,1,0:T(8,128)} async-done(((f32[2,32,128]{2,1,0:T(8,128)}), f32[64,32,128]{2,1,0:T(8,128)}) %all-gather.10.cloned.1.call-update) | async-done | bytes 1048592 | tf_op jit(solution)/shard_map/all_gather | solution.py:34
  269.3 15.3 %while.31 = (s32[]{:T(128)}, f32[32,32,128]{2,0,1:T(8,128)S(1)}, s32[]{:T(128)}, s32[32]{0:T(128)S(1)}, s32[]{:T(128)}, /*index=5*/s32[32]{0:T(128)S(1)}, f32[64...) while((s32[]{:T(128)}, f32[32,32,128]{2,0,1:T(8,128)S(1)}, ...), condition=%wide.region_4.6_spmd, body=%wide.region_3.5_spmd.sunk | while | flops 63080028 | bytes 2232807 | solution.py:30
  269.3 0.8 compare_and_fusion.7
  270.2 1.8 gather_fusion.1
  271.9 1.7 fusion.80
  273.7 0.8 convolution_add_fusion.7
  274.5 0.7 compare_and_fusion.7
  275.2 1.8 gather_fusion.1
  277.0 1.7 fusion.80
  278.7 0.8 convolution_add_fusion.7
  279.6 0.7 compare_and_fusion.7
  280.3 1.8 gather_fusion.1
  282.1 1.7 fusion.80
  283.8 0.8 convolution_add_fusion.7
  284.6 1.1 copy.26
  285.8 90.4 %reduce-scatter.5.cloned.1.call-done = f32[1,1,2,32,128]{4,3,2,1,0:T(8,128)} async-done(((f32[1,16,2,32,128]{4,3,2,1,0:T(8,128)}), f32[1,1,2,32,128]{4,3,2,1,0:T(8,128)}) %reduce-scatter.5.cloned.1.call-update) | async-done | bytes 32784 | tf_op jit(solution)/shard_map/reduce_scatter | solution.py:49
  376.2 1.4 sub.30
  378.3 0.8 fusion.52
  379.2 67.5 %all-gather.6.cloned.1.call-done = f32[32,1,2,32,128]{4,3,2,1,0:T(8,128)} async-done(((f32[1,1,2,32,128]{4,3,2,1,0:T(8,128)}), f32[32,1,2,32,128]{4,3,2,1,0:T(8,128)}) %all-gather.6.cloned.1.call-update) | async-done | bytes 1048592 | tf_op jit(solution)/shard_map/all_gather | solution.py:34
  446.8 3.6 while.32
  446.8 0.7 compare_and_fusion.8
  447.5 1.8 gather_fusion.2
  449.3 0.6 fusion.85
  450.0 0.3 convolution_add_fusion.8
  450.4 0.3 fusion.44
  450.7 82.6 %psum.7 = f32[1,2,32,128]{3,2,1,0:T(8,128)} all-reduce(f32[1,2,32,128]{3,2,1,0:T(8,128)S(1)} %fusion.44), channel_id=1, replica_groups=mesh['row'=32,'col'=16] {'col'}, use_global_device_ids=true, to_apply=%region_8.10 | all-reduce | flops 8192 | bytes 65536 | tf_op jit(solution)/shard_map/psum | solution.py:99
  (46 shorter events, 0.8 us)
Async XLA Ops:
  7.2 0.9 copy-start
  7.2 79.4 %all-gather.8.cloned.1.call-start = ((), (), s32[]{:S(2)}) async-start(), calls=%async_computation.5 | async-start | bytes 1081344 | tf_op jit(solution)/shard_map/all_gather | solution.py:34
  9.7 189.1 %reduce-scatter.3.cloned.1.call-start = ((), (), s32[]{:S(2)}) async-start(), calls=%async_computation.2 | async-start | bytes 557056 | tf_op jit(solution)/shard_map/reduce_scatter | solution.py:49
  86.7 112.1 %copy-start.2 = (f32[1,1,2,32,128]{4,3,2,1,0:T(8,128)S(1)}, f32[1,1,2,32,128]{4,3,2,1,0:T(8,128)}, u32[]{:S(2)}) copy-start(f32[1,1,2,32,128]{4,3,2,1,0:T(8,128)} %param.20) | copy-start | bytes 98308
  86.7 112.1 %copy-start.3 = (f32[2,32,128]{2,1,0:T(8,128)S(1)}, f32[2,32,128]{2,1,0:T(8,128)}, u32[]{:S(2)}) copy-start(f32[2,32,128]{2,1,0:T(8,128)} %convolution_multiply_fusion.1) | copy-start | bytes 98308
  105.8 163.4 %copy-start.4 = (s32[32]{0:T(128)S(1)}, s32[32]{0:T(128)}, u32[]{:S(2)}) copy-start(s32[32]{0:T(128)} %get-tuple-element.489) | copy-start | bytes 388
  105.9 163.4 %copy-start.8 = (s32[32]{0:T(128)S(1)}, s32[32]{0:T(128)}, u32[]{:S(2)}) copy-start(s32[32]{0:T(128)} %get-tuple-element.491) | copy-start | bytes 388
  107.0 162.2 %all-gather.10.cloned.1.call-start = ((), (), s32[]{:S(2)}) async-start(), calls=%async_computation.6 | async-start | bytes 1081344 | tf_op jit(solution)/shard_map/all_gather | solution.py:34
  200.4 175.8 %reduce-scatter.5.cloned.1.call-start = ((), (), s32[]{:S(2)}) async-start(), calls=%async_computation.3 | async-start | bytes 557056 | tf_op jit(solution)/shard_map/reduce_scatter | solution.py:49
  269.3 109.0 %copy-start.6 = (f32[1,1,2,128]{3,2,1,0:T(2,128)S(1)}, f32[1,1,2,128]{3,2,1,0:T(2,128)}, u32[]{:S(2)}) copy-start(f32[1,1,2,128]{3,2,1,0:T(2,128)} %param.30) | copy-start | bytes 3076
  269.3 177.4 %copy-start.1 = (f32[1,1,16,128,128]{4,3,2,1,0:T(8,128)S(1)}, f32[1,1,16,128,128]{4,3,2,1,0:T(8,128)}, u32[]{:S(2)}) copy-start(f32[1,1,16,128,128]{4,3,2,1,0:T(8,128)} %param.26) | copy-start | bytes 3145732
  269.3 177.4 %copy-start.5 = (s32[1,1,16]{2,1,0:T(1,128)S(1)}, s32[1,1,16]{2,1,0:T(1,128)}, u32[]{:S(2)}) copy-start(s32[1,1,16]{2,1,0:T(1,128)} %param.28) | copy-start | bytes 196
  269.3 177.4 %copy-start.9 = (s32[1,1,16]{2,1,0:T(1,128)S(1)}, s32[1,1,16]{2,1,0:T(1,128)}, u32[]{:S(2)}) copy-start(s32[1,1,16]{2,1,0:T(1,128)} %param.27) | copy-start | bytes 196
  285.8 160.9 %all-gather.6.cloned.1.call-start = ((), (), s32[]{:S(2)}) async-start(), calls=%async_computation.4 | async-start | bytes 1081344 | tf_op jit(solution)/shard_map/all_gather | solution.py:34
  446.7 3.6 copy-start.7
Sparse Core Ops, SparseCore 0:
  11.7 74.8 all-gather.7
  107.1 91.6 reduce-scatter.2
  202.5 66.6 all-gather.9
  285.9 90.2 reduce-scatter.4
  379.8 66.8 all-gather.5
where the time goes:
time: 541 us; the launch traced here: 540 us
  waiting for transfers between devices  395 us (73%)
  blocking collectives  82.6 us (15%)
  matrix products  19.1 us (4%)
  local copies, waits for them, and re-layouts  18.2 us (3%)
  between operations  15.3 us (3%)
  other arithmetic  9.33 us (2%)
    all_gather x3, waiting for transfers between devices, gather_columns(): whole = lax.all_gather(vec[None, None], 'row', axis=0, tiled=True)  212 us
    reduce_scatter x2, waiting for transfers between devices, stiffness_product(): lax.psum_scatter(partial_value, 'col', scatter_dimension=1, tiled=True)  182 us
    psum x1, blocking collectives, body(): coarse = lax.psum(part, 'col')  82.6 us
    gather x7, local copies, waits for them, and re-layouts, add_group(): inputs = jnp.take(blocks, col_ids, axis=0)  12.5 us
  transfers between devices with their start and end apart: 5, of which 5 were waited for; matrix products, arithmetic and copies ran while one was open for 0% of the time, Pallas kernels for 0%

commit v1 on v0

--- a/solution.py
+++ b/solution.py
@@ -6,6 +6,13 @@
 omega = 0.7
 highest = lax.Precision.HIGHEST
 tile_group = 8
+
+
+def exchange_gather(shard, name, d):
+    size = lax.axis_size(name)
+    pieces = jnp.stack([shard for _ in range(size)])
+    pieces = lax.all_to_all(pieces, name, split_axis=0, concat_axis=0)
+    return jnp.concatenate(pieces, axis=d)
 
 
 def loop_tiles(blocks, stiffness_submatrices, rows, cols, low, high, nout):
@@ -31,7 +38,7 @@
 
 
 def gather_columns(vec):
-    whole = lax.all_gather(vec[None, None], "row", axis=0, tiled=True)
+    whole = exchange_gather(vec[None, None], "row", 0)
     return whole.reshape(-1, vec.shape[1], vec.shape[2])
 
 

time: 541 us -> 496 us (0.917)
  the two profiles are of different devices: /device:TPU:8 before, /device:TPU:128 now
where the time goes in v1:
time: 496 us; the launch traced here: 495 us
  waiting for transfers between devices  317 us (64%)
  blocking collectives  82.2 us (17%)
  starting transfers between devices  41.2 us (8%)
  local copies, waits for them, and re-layouts  20.4 us (4%)
  between operations  15.6 us (3%)
  matrix products  11.6 us (2%)
  other arithmetic  5.99 us (1%)
    reduce_scatter x2, waiting for transfers between devices, stiffness_product(): lax.psum_scatter(partial_value, 'col', scatter_dimension=1, tiled=True)  183 us
    all_to_all x3, waiting for transfers between devices, exchange_gather(): pieces = lax.all_to_all(pieces, name, split_axis=0, concat_axis=0)  134 us
    psum x1, blocking collectives, body(): coarse = lax.psum(part, 'col')  82.2 us
    all_to_all x3, starting transfers between devices, exchange_gather(): pieces = lax.all_to_all(pieces, name, split_axis=0, concat_axis=0)  41.1 us
    gather x7, local copies, waits for them, and re-layouts, add_group(): inputs = jnp.take(blocks, col_ids, axis=0)  11.2 us
  transfers between devices with their start and end apart: 5, of which 5 were waited for; matrix products, arithmetic and copies ran while one was open for 0% of the time, Pallas kernels for 0%

profile of v1, /device:TPU:128, one launch (start us, length us, event | category | flops | bytes accessed | tf_op | source)
XLA Modules:
  0.0 494.8 jit_solution(5748546671955443597)
XLA Ops:
  7.2 0.9 copy-done
  8.1 1.0 convolution_multiply_fusion.1
  9.1 1.1 stack.9
  10.2 16.6 %all-to-all-start = ((f32[32,1,1,2,32,128]{5,4,3,2,1,0:T(8,128)}), f32[32,1,1,2,32,128]{5,4,3,2,1,0:T(8,128)S(1)}, u32[]{:S(2)}, u32[]{:S(2)}) async-start(f32[32,1,1,2,32,128]{5,4,3,2,1,0:T(8,128)} %stack.9), calls=%async_computation | async-start | bytes 2097152 | tf_op jit(solution)/shard_map/all_to_all | solution.py:14
  27.5 49.8 %all-to-all-done = f32[32,1,1,2,32,128]{5,4,3,2,1,0:T(8,128)S(1)} async-done(((f32[32,1,1,2,32,128]{5,4,3,2,1,0:T(8,128)}), f32[32,1,1,2,32,128]{5,4,3,2,1,0:T(8,128)S(1)}, u32[]{:S(2)}, u32[]{:S(2)}) %all-to-all-start) | async-done | bytes 1048608 | tf_op jit(solution)/shard_map/all_to_all | solution.py:14
  77.4 1.0 copy-done.3
  78.4 12.1 %while.30 = (s32[]{:T(128)}, f32[32,32,128]{2,0,1:T(8,128)S(1)}, s32[]{:T(128)}, s32[32]{0:T(128)S(1)}, s32[]{:T(128)}, /*index=5*/s32[32]{0:T(128)S(1)}, f32[64...) while((s32[]{:T(128)}, f32[32,32,128]{2,0,1:T(8,128)S(1)}, ...), condition=%wide.region_1.3_spmd, body=%wide.region_0.2_spmd.sunk | while | flops 63080028 | bytes 2233311 | solution.py:37
  78.5 0.7 compare_and_fusion.6
  79.2 1.8 gather_fusion
  81.0 0.6 fusion.75
  81.7 0.8 convolution_add_fusion.6
  82.5 0.7 compare_and_fusion.6
  83.2 1.8 gather_fusion
  85.0 0.6 fusion.75
  85.7 0.8 convolution_add_fusion.6
  86.5 0.7 compare_and_fusion.6
  87.3 1.8 gather_fusion
  89.0 0.6 fusion.75
  89.7 0.8 convolution_add_fusion.6
  90.5 1.1 copy.25
  91.7 91.2 %reduce-scatter.3.cloned.1.call-done = f32[1,1,2,32,128]{4,3,2,1,0:T(8,128)} async-done(((f32[1,16,2,32,128]{4,3,2,1,0:T(8,128)}), f32[1,1,2,32,128]{4,3,2,1,0:T(8,128)}) %reduce-scatter.3.cloned.1.call-update) | async-done | bytes 32784 | tf_op jit(solution)/shard_map/reduce_scatter | solution.py:56
  182.9 1.0 fusion.45
  183.9 1.1 stack.10
  185.0 12.2 %all-to-all-start.1 = ((f32[32,1,1,2,32,128]{5,4,3,2,1,0:T(8,128)}), f32[32,1,1,2,32,128]{5,4,3,2,1,0:T(8,128)S(1)}, u32[]{:S(2)}, u32[]{:S(2)}) async-start(f32[32,1,1,2,32,128]{5,4,3,2,1,0:T(8,128)} %stack.10), calls=%async_computation.2 | async-start | bytes 2097152 | tf_op jit(solution)/shard_map/all_to_all | solution.py:14
  197.3 42.5 %all-to-all-done.1 = f32[32,1,1,2,32,128]{5,4,3,2,1,0:T(8,128)S(1)} async-done(((f32[32,1,1,2,32,128]{5,4,3,2,1,0:T(8,128)}), f32[32,1,1,2,32,128]{5,4,3,2,1,0:T(8,128)S(1)}, u32[]{:S(2)}, u32[]{:S(2)}) %all-to-all-start.1) | async-done | bytes 1048608 | tf_op jit(solution)/shard_map/all_to_all | solution.py:14
  239.8 1.0 copy-done.4
  240.8 12.1 %while.31 = (s32[]{:T(128)}, f32[32,32,128]{2,0,1:T(8,128)S(1)}, s32[]{:T(128)}, s32[32]{0:T(128)S(1)}, s32[]{:T(128)}, /*index=5*/s32[32]{0:T(128)S(1)}, f32[64...) while((s32[]{:T(128)}, f32[32,32,128]{2,0,1:T(8,128)S(1)}, ...), condition=%wide.region_4.6_spmd, body=%wide.region_3.5_spmd.sunk | while | flops 63080028 | bytes 2233311 | solution.py:37
  240.9 0.7 compare_and_fusion.7
  241.6 1.8 gather_fusion.1
  243.4 0.6 fusion.80
  244.1 0.8 convolution_add_fusion.7
  244.9 0.7 compare_and_fusion.7
  245.6 1.8 gather_fusion.1
  247.4 0.6 fusion.80
  248.1 0.8 convolution_add_fusion.7
  248.9 0.7 compare_and_fusion.7
  249.6 1.8 gather_fusion.1
  252.1 0.8 convolution_add_fusion.7
  252.9 1.1 copy.26
  254.1 92.2 %reduce-scatter.5.cloned.1.call-done = f32[1,1,2,32,128]{4,3,2,1,0:T(8,128)} async-done(((f32[1,16,2,32,128]{4,3,2,1,0:T(8,128)}), f32[1,1,2,32,128]{4,3,2,1,0:T(8,128)}) %reduce-scatter.5.cloned.1.call-update) | async-done | bytes 32784 | tf_op jit(solution)/shard_map/reduce_scatter | solution.py:56
  346.3 0.8 sub.34
  347.1 1.1 stack.11
  348.2 12.3 %all-to-all-start.2 = ((f32[32,1,1,2,32,128]{5,4,3,2,1,0:T(8,128)}), f32[32,1,1,2,32,128]{5,4,3,2,1,0:T(8,128)S(1)}, u32[]{:S(2)}, u32[]{:S(2)}) async-start(f32[32,1,1,2,32,128]{5,4,3,2,1,0:T(8,128)} %stack.11), calls=%async_computation.4 | async-start | bytes 2097152 | tf_op jit(solution)/shard_map/all_to_all | solution.py:14
  361.3 41.7 %all-to-all-done.2 = f32[32,1,1,2,32,128]{5,4,3,2,1,0:T(8,128)S(1)} async-done(((f32[32,1,1,2,32,128]{5,4,3,2,1,0:T(8,128)}), f32[32,1,1,2,32,128]{5,4,3,2,1,0:T(8,128)S(1)}, u32[]{:S(2)}, u32[]{:S(2)}) %all-to-all-start.2) | async-done | bytes 1048608 | tf_op jit(solution)/shard_map/all_to_all | solution.py:14
  403.1 2.4 while.32
  403.1 0.7 compare_and_fusion.8
  404.4 0.6 fusion.85
  405.8 82.2 %psum.7 = f32[1,2,32,128]{3,2,1,0:T(8,128)} all-reduce(f32[1,2,32,128]{3,2,1,0:T(8,128)S(1)} %fusion.44), channel_id=1, replica_groups=mesh['row'=32,'col'=16] {'col'}, use_global_device_ids=true, to_apply=%region_8.10 | all-reduce | flops 8192 | bytes 65536 | tf_op jit(solution)/shard_map/psum | solution.py:106
  (56 shorter events, 2.7 us)
Async XLA Ops:
  7.2 0.9 copy-start
  7.2 71.2 %copy-start.13 = (s32[1,1,32]{2,1,0:T(1,128)S(1)}, s32[1,1,32]{2,1,0:T(1,128)}, u32[]{:S(2)}) copy-start(s32[1,1,32]{2,1,0:T(1,128)} %param.23) | copy-start | bytes 388
  7.2 71.2 %copy-start.9 = (s32[1,1,32]{2,1,0:T(1,128)S(1)}, s32[1,1,32]{2,1,0:T(1,128)}, u32[]{:S(2)}) copy-start(s32[1,1,32]{2,1,0:T(1,128)} %param.24) | copy-start | bytes 388
  7.2 71.2 %copy-start.1 = (f32[1,1,32,128,128]{4,3,2,1,0:T(8,128)S(1)}, f32[1,1,32,128,128]{4,3,2,1,0:T(8,128)}, u32[]{:S(2)}) copy-start(f32[1,1,32,128,128]{4,3,2,1,0:T(8,128)} %param.22) | copy-start | bytes 6291460
  10.2 67.2 %all-to-all-start = ((f32[32,1,1,2,32,128]{5,4,3,2,1,0:T(8,128)}), f32[32,1,1,2,32,128]{5,4,3,2,1,0:T(8,128)S(1)}, u32[]{:S(2)}, u32[]{:S(2)}) async-start(f32[32,1,1,2,32,128]{5,4,3,2,1,0:T(8,128)} %stack.9), calls=%async_computation | async-start | bytes 2097152 | tf_op jit(solution)/shard_map/all_to_all | solution.py:14
  26.8 156.1 %reduce-scatter.3.cloned.1.call-start = ((), (), s32[]{:S(2)}) async-start(), calls=%async_computation.5 | async-start | bytes 557056 | tf_op jit(solution)/shard_map/reduce_scatter | solution.py:56
  77.3 1.0 copy-start.3
  78.4 104.5 %copy-start.5 = (f32[1,1,2,32,128]{4,3,2,1,0:T(8,128)S(1)}, f32[1,1,2,32,128]{4,3,2,1,0:T(8,128)}, u32[]{:S(2)}) copy-start(f32[1,1,2,32,128]{4,3,2,1,0:T(8,128)} %param.20) | copy-start | bytes 98308
  183.9 56.9 %copy-start.8 = (f32[2,32,128]{2,1,0:T(8,128)}, f32[2,32,128]{2,1,0:T(8,128)S(1)}, u32[]{:S(2)}) copy-start(f32[2,32,128]{2,1,0:T(8,128)S(1)} %fusion.45) | copy-start | bytes 98308
  185.0 54.7 %all-to-all-start.1 = ((f32[32,1,1,2,32,128]{5,4,3,2,1,0:T(8,128)}), f32[32,1,1,2,32,128]{5,4,3,2,1,0:T(8,128)S(1)}, u32[]{:S(2)}, u32[]{:S(2)}) async-start(f32[32,1,1,2,32,128]{5,4,3,2,1,0:T(8,128)} %stack.10), calls=%async_computation.2 | async-start | bytes 2097152 | tf_op jit(solution)/shard_map/all_to_all | solution.py:14
  197.3 149.0 %reduce-scatter.5.cloned.1.call-start = ((), (), s32[]{:S(2)}) async-start(), calls=%async_computation.6 | async-start | bytes 557056 | tf_op jit(solution)/shard_map/reduce_scatter | solution.py:56
  239.8 1.0 copy-start.4
  254.0 107.2 %copy-start.11 = (f32[1,1,2,128]{3,2,1,0:T(2,128)S(1)}, f32[1,1,2,128]{3,2,1,0:T(2,128)}, u32[]{:S(2)}) copy-start(f32[1,1,2,128]{3,2,1,0:T(2,128)} %param.30) | copy-start | bytes 3076
  254.0 149.0 %copy-start.2 = (f32[1,1,16,128,128]{4,3,2,1,0:T(8,128)S(1)}, f32[1,1,16,128,128]{4,3,2,1,0:T(8,128)}, u32[]{:S(2)}) copy-start(f32[1,1,16,128,128]{4,3,2,1,0:T(8,128)} %param.26) | copy-start | bytes 3145732
  254.0 149.0 %copy-start.10 = (s32[1,1,16]{2,1,0:T(1,128)S(1)}, s32[1,1,16]{2,1,0:T(1,128)}, u32[]{:S(2)}) copy-start(s32[1,1,16]{2,1,0:T(1,128)} %param.28) | copy-start | bytes 196
  254.0 149.0 %copy-start.14 = (s32[1,1,16]{2,1,0:T(1,128)S(1)}, s32[1,1,16]{2,1,0:T(1,128)}, u32[]{:S(2)}) copy-start(s32[1,1,16]{2,1,0:T(1,128)} %param.27) | copy-start | bytes 196
  346.3 14.9 %copy-start.7 = (f32[1,1,2,32,128]{4,3,2,1,0:T(8,128)S(1)}, f32[1,1,2,32,128]{4,3,2,1,0:T(8,128)}, u32[]{:S(2)}) copy-start(f32[1,1,2,32,128]{4,3,2,1,0:T(8,128)} %reduce-scatter.5.cloned.1.call-done) | copy-start | bytes 98308
  347.1 56.0 %copy-start.6 = (f32[1,1,2,32,128]{4,3,2,1,0:T(8,128)}, f32[1,1,2,32,128]{4,3,2,1,0:T(8,128)S(1)}, u32[]{:S(2)}) copy-start(f32[1,1,2,32,128]{4,3,2,1,0:T(8,128)S(1)} %sub.34) | copy-start | bytes 98308
  348.2 54.8 %all-to-all-start.2 = ((f32[32,1,1,2,32,128]{5,4,3,2,1,0:T(8,128)}), f32[32,1,1,2,32,128]{5,4,3,2,1,0:T(8,128)S(1)}, u32[]{:S(2)}, u32[]{:S(2)}) async-start(f32[32,1,1,2,32,128]{5,4,3,2,1,0:T(8,128)} %stack.11), calls=%async_computation.4 | async-start | bytes 2097152 | tf_op jit(solution)/shard_map/all_to_all | solution.py:14
  403.1 2.4 copy-start.12
Sparse Core Ops, SparseCore 0:
  91.8 91.0 reduce-scatter.2
  254.2 92.0 reduce-scatter.4
